TPU v7x, 256 devices: a whole 4x4x8 slice. The times are simulated.
256 devices in a mesh: tile: 128 (over y, z, x), sub: 2 (over core).
Axes of the slice: x: 4, y: 4, z: 8, core: 2. Of those that a mesh axis runs over, the one named last changes fastest.
Arguments:
- right_side: float32 [2, 32768, 256], P(None, ('tile', 'sub')), may hold values from -12 to 12
- pixel_weight: float32 [32768, 256], P(('tile', 'sub')), may hold values from 0.5 to 2
- noise_diag: float32 [2, 32768, 256], P(None, ('tile', 'sub')), may hold values from 0.5 to 8
- noise_corr: float32 [32768, 256], P(('tile', 'sub')), may hold values from -0.8 to 0.8
- neighbours: int32 [3, 4, 128], replicated, may hold values from 0 to 127, as said below
Outputs:
- solution: float32 [2, 32768, 256], P(None, ('tile', 'sub'))
- final_misfit: float32 [2, 32768, 256], P(None, ('tile', 'sub'))
Inputs may be any that keep to these rules, and one draw needn't show every extreme that they name: `neighbours`: across side 0 lies side 1 of another or the same tile and across side 2 lies side 3, and conversely; the relation is symmetric, with the same reversal flag on both sides of an edge. Every neighbour lies, in the cyclic order of tiles, within 3 places of its tile or within 3 places of the tile 128/2 places away, and 3 places is reached. Flags are 0 or 1.
All inputs are finite; a program needn't handle non-finite values.
Results may differ from a plain program's by a relative error of at most 0.00012.
Values sent between devices are 32-bit elements; how exact they have to be, the bound alone decides.
A program may use at most 128 MiB of HBM per device.

v0:
```python
import jax
import jax.numpy as jnp
from jax import lax
from jax.sharding import PartitionSpec as P

NU = 2
NC = 3
MASS = 0.05
OMEGA = 0.8


def with_halo(block, sides, width):
    for axis, dim in sides:
        count = lax.axis_size(axis)
        forward = [(i, i + 1) for i in range(count - 1)]
        backward = [(target, source) for source, target in forward]
        low = lax.ppermute(
            lax.slice_in_dim(block, block.shape[dim] - width, None, axis=dim), axis, forward
        )
        high = lax.ppermute(lax.slice_in_dim(block, 0, width, axis=dim), axis, backward)
        block = jnp.concatenate([low, block, high], axis=dim)
    return block


def inverse_blocks(diag_term, noise_terms):
    upper_left = diag_term + noise_terms[0]
    lower_right = diag_term + noise_terms[1]
    determinant = upper_left * lower_right - noise_terms[2] * noise_terms[2]
    return jnp.stack(
        [lower_right / determinant, upper_left / determinant, -noise_terms[2] / determinant]
    )


def apply_block(inverse, misfit):
    out_first = inverse[0] * misfit[0] + inverse[2] * misfit[1]
    second = inverse[2] * misfit[0] + inverse[1] * misfit[1]
    return jnp.stack([out_first, second])


def coarsen_sum(values):
    old_shape = values.shape
    new_shape = old_shape[:-2] + (old_shape[-2] // 2, 2, old_shape[-1] // 2, 2)
    return values.reshape(new_shape).sum(axis=(-3, -1))


def prolong(values):
    return jnp.repeat(jnp.repeat(values, 2, axis=-2), 2, axis=-1)


def across_sides(side_rows, link_cols, grid_level):
    if grid_level == "fine":
        everyone = lax.all_gather(side_rows[None], "tile", axis=0, tiled=True)
    else:
        everyone = lax.all_gather(side_rows[None], "tile", axis=0, tiled=True)
    across = everyone[link_cols[0], link_cols[1]]
    flipped = jnp.flip(across, axis=2)
    return jnp.where(link_cols[2][:, None, None] == 1, flipped, across)


def band_sum(scaled, link_cols, grid_level):
    sub_id = lax.axis_index("sub")
    sub_count = lax.axis_size("sub")
    band_rows = scaled.shape[1]
    band_width = scaled.shape[2]
    if grid_level == "fine":
        padded = with_halo(scaled, (("sub", 1),), 1)
    else:
        padded = with_halo(scaled, (("sub", 1),), 1)
    zeros_row = jnp.zeros((2, band_width), jnp.float32)
    start_row = (jnp.int32(0), sub_id * band_rows)
    top_part = jnp.where(sub_id == 0, scaled[:, 0, :], zeros_row)
    bottom_part = jnp.where(sub_id == sub_count - 1, scaled[:, band_rows - 1, :], zeros_row)
    left_part = lax.dynamic_update_slice(zeros_row, scaled[:, :, 0], start_row)
    right_part = lax.dynamic_update_slice(zeros_row, scaled[:, :, band_width - 1], start_row)
    partial_sides = jnp.stack([top_part, bottom_part, left_part, right_part])
    if grid_level == "fine":
        side_rows = lax.psum(partial_sides, "sub")
    else:
        side_rows = lax.psum(partial_sides, "sub")
    across = across_sides(side_rows, link_cols, grid_level)
    upper_row = padded[:, 0, :] + jnp.where(sub_id == 0, across[0], zeros_row)
    lower_row = padded[:, band_rows + 1, :] + jnp.where(
        sub_id == sub_count - 1, across[1], zeros_row
    )
    left_col = lax.dynamic_slice(across[2], start_row, (2, band_rows))
    right_col = lax.dynamic_slice(across[3], start_row, (2, band_rows))
    above_rows = jnp.concatenate([upper_row[:, None, :], scaled[:, :-1, :]], axis=1)
    below_rows = jnp.concatenate([scaled[:, 1:, :], lower_row[:, None, :]], axis=1)
    west_cols = jnp.concatenate([left_col[:, :, None], scaled[:, :, :-1]], axis=2)
    east_cols = jnp.concatenate([scaled[:, :, 1:], right_col[:, :, None]], axis=2)
    return above_rows + below_rows + west_cols + east_cols


def operate(iterate, weight, stiffness, noise_terms, link_cols, grid_level):
    scaled = weight * iterate
    beside_all = band_sum(scaled, link_cols, grid_level)
    stencil = (MASS + 4.0) * scaled - beside_all
    out_first = (
        stiffness * weight * stencil[0] + noise_terms[0] * iterate[0] + noise_terms[2] * iterate[1]
    )
    second = (
        stiffness * weight * stencil[1] + noise_terms[2] * iterate[0] + noise_terms[1] * iterate[1]
    )
    return jnp.stack([out_first, second])


def relax(iterate, source, weight, stiffness, noise_terms, inverse, link_cols, grid_level):
    misfit = source - operate(iterate, weight, stiffness, noise_terms, link_cols, grid_level)
    return iterate + OMEGA * apply_block(inverse, misfit)


def coarse_solve(coarse_source, coarse_weight, coarse_noise, link_cols):
    coarse_inverse = inverse_blocks(
        2.0 * (MASS + 4.0) * coarse_weight * coarse_weight, coarse_noise
    )
    correction = OMEGA * apply_block(coarse_inverse, coarse_source)
    for sweep_no in range(NC - 1):
        correction = relax(
            correction,
            coarse_source,
            coarse_weight,
            2.0,
            coarse_noise,
            coarse_inverse,
            link_cols,
            "coarse",
        )
    return correction


def body(right_side, pixel_weight, noise_diag, noise_corr, neighbours):
    link_cols = lax.dynamic_slice_in_dim(neighbours, lax.axis_index("tile"), 1, 2)[:, :, 0]
    cross_noise = noise_corr * jnp.sqrt(noise_diag[0] * noise_diag[1])
    noise_terms = jnp.stack([noise_diag[0], noise_diag[1], cross_noise])
    inverse = inverse_blocks((MASS + 4.0) * pixel_weight * pixel_weight, noise_terms)
    iterate = OMEGA * apply_block(inverse, right_side)
    iterate = relax(iterate, right_side, pixel_weight, 1.0, noise_terms, inverse, link_cols, "fine")
    misfit = right_side - operate(iterate, pixel_weight, 1.0, noise_terms, link_cols, "fine")
    coarse_source = coarsen_sum(misfit)
    coarse_weight = 0.25 * coarsen_sum(pixel_weight)
    coarse_noise = coarsen_sum(noise_terms)
    correction = coarse_solve(coarse_source, coarse_weight, coarse_noise, link_cols)
    iterate = iterate + prolong(correction)
    for sweep_no in range(NU):
        iterate = relax(
            iterate, right_side, pixel_weight, 1.0, noise_terms, inverse, link_cols, "fine"
        )
    final_misfit = right_side - operate(iterate, pixel_weight, 1.0, noise_terms, link_cols, "fine")
    return (iterate, final_misfit)


def solution(mesh):
    placed = (
        P(None, ("tile", "sub"), None),
        P(("tile", "sub"), None),
        P(None, ("tile", "sub"), None),
        P(("tile", "sub"), None),
        P(),
    )
    return jax.shard_map(
        body,
        mesh=mesh,
        in_specs=placed,
        out_specs=(P(None, ("tile", "sub"), None), P(None, ("tile", "sub"), None)),
        check_vma=False,
    )
```

profile of v0, /device:TPU:2, one launch (start us, length us, event | category | flops | bytes accessed | tf_op | source)
XLA Modules:
  0.0 1307.8 jit_solution(11690635591361222974)
XLA Ops:
  15.5 3.1 psum.49
  20.0 3.7 collective-permute-start
  28.3 96.1 %all-gather.6.cloned.1.call-done = f32[128,4,2,256]{3,1,2,0:T(4,128)} async-done(((f32[1,4,2,256]{3,1,2,0:T(4,128)}), f32[128,4,2,256]{3,1,2,0:T(4,128)}) %all-gather.6.cloned.1.call-update) | async-done | bytes 1048592 | tf_op jit(solution)/shard_map/all_gather | solution.py:52
  124.4 2.8 copy.1535
  127.1 1.8 gather_fusion
  130.8 2.0 fusion.2
  134.6 3.1 psum.50
  137.8 9.8 stack.205
  147.6 18.0 %stack.204 = f32[2,64,2,128,2]{4,3,2,1,0:T(8,128)} reshape(f32[2,128,256]{2,1,0:T(8,128)S(1)} %copy-done.1) | data formatting | bytes 524288 | tf_op jit(solution)/shard_map/stack | solution.py:134
  165.6 9.7 reshape.563
  175.3 4.5 reduce_sum.27
  180.5 12.0 maximum_reduce_fusion
  192.5 2.1 collective-permute-start.2
  197.7 41.9 %all-gather.8.cloned.1.call-done = f32[128,4,2,256]{3,1,2,0:T(4,128)} async-done(((f32[1,4,2,256]{3,1,2,0:T(4,128)}), f32[128,4,2,256]{3,1,2,0:T(4,128)}) %all-gather.8.cloned.1.call-update) | async-done | bytes 1048592 | tf_op jit(solution)/shard_map/all_gather | solution.py:52
  239.6 1.8 copy.1556
  244.0 18.1 %reshape.564 = f32[2,64,2,128,2]{4,3,2,1,0:T(8,128)} reshape(f32[2,128,256]{2,1,0:T(8,128)S(1)} %maximum_subtract_fusion.1) | data formatting | bytes 524288 | tf_op jit(solution)/shard_map/reshape | solution.py:43
  262.1 8.0 reduce_sum.29
  273.4 3.4 psum.51
  276.9 341.1 %all_gather.23 = f32[128,4,2,128]{3,1,2,0:T(4,128)S(1)} all-gather(f32[1,4,2,128]{3,1,2,0:T(4,128)S(1)} %copy.1565), channel_id=1, replica_groups=mesh['tile'=128,'sub'=2] {'tile'}, dimensions={0}, use_global_device_ids=true | all-gather | bytes 528384 | tf_op jit(solution)/shard_map/all_gather | solution.py:54
  621.1 3.0 collective-permute-start.6
  624.6 2.5 psum.52
  627.1 347.0 %all_gather.24 = f32[128,4,2,128]{3,1,2,0:T(4,128)S(1)} all-gather(f32[1,4,2,128]{3,1,2,0:T(4,128)S(1)} %copy.1573), channel_id=1, replica_groups=mesh['tile'=128,'sub'=2] {'tile'}, dimensions={0}, use_global_device_ids=true | all-gather | bytes 528384 | tf_op jit(solution)/shard_map/all_gather | solution.py:54
  976.6 3.1 psum.53
  979.8 2.1 collective-permute-start.8
  984.8 89.8 %all-gather.10.cloned.1.call-done = f32[128,4,2,256]{3,1,2,0:T(4,128)} async-done(((f32[1,4,2,256]{3,1,2,0:T(4,128)}), f32[128,4,2,256]{3,1,2,0:T(4,128)}) %all-gather.10.cloned.1.call-update) | async-done | bytes 1048592 | tf_op jit(solution)/shard_map/all_gather | solution.py:52
  1074.6 1.8 copy.1587
  1079.9 3.1 psum.54
  1083.1 2.1 collective-permute-start.10
  1088.3 96.6 %all-gather.12.cloned.1.call-done = f32[128,4,2,256]{3,1,2,0:T(4,128)} async-done(((f32[1,4,2,256]{3,1,2,0:T(4,128)}), f32[128,4,2,256]{3,1,2,0:T(4,128)}) %all-gather.12.cloned.1.call-update) | async-done | bytes 1048592 | tf_op jit(solution)/shard_map/all_gather | solution.py:52
  1190.6 3.1 psum.55
  1195.0 3.0 collective-permute-start.12
  1199.2 96.3 %all-gather.14.cloned.1.call-done = f32[128,4,2,256]{3,1,2,0:T(4,128)} async-done(((f32[1,4,2,256]{3,1,2,0:T(4,128)}), f32[128,4,2,256]{3,1,2,0:T(4,128)}) %all-gather.14.cloned.1.call-update) | async-done | bytes 1048592 | tf_op jit(solution)/shard_map/all_gather | solution.py:52
  (276 shorter events, 56.1 us)
Async XLA Ops:
  7.2 126.2 %copy-start = (f32[128,256]{1,0:T(8,128)S(1)}, f32[128,256]{1,0:T(8,128)}, u32[]{:S(2)}) copy-start(f32[128,256]{1,0:T(8,128)} %param.6) | copy-start | bytes 393220
  7.2 140.4 %copy-start.1 = (f32[2,128,256]{2,1,0:T(8,128)S(1)}, f32[2,128,256]{2,1,0:T(8,128)}, u32[]{:S(2)}) copy-start(f32[2,128,256]{2,1,0:T(8,128)} %param.7) | copy-start | bytes 786436
  7.2 117.2 %all-gather.6.cloned.1.call-start = ((), (), s32[]{:S(2)}) async-start(), calls=%async_computation | async-start | bytes 1056768 | tf_op jit(solution)/shard_map/all_gather | solution.py:52
  18.6 220.9 %all-gather.8.cloned.1.call-start = ((), (), s32[]{:S(2)}) async-start(), calls=%async_computation.1 | async-start | bytes 1056768 | tf_op jit(solution)/shard_map/all_gather | solution.py:52
  18.7 111.0 %collective-permute-start.1 = (f32[2,1,256]{1,0,2:T(2,128)}, f32[2,1,256]{1,0,2:T(2,128)}, u32[]{:S(2)}, u32[]{:S(2)}) collective-permute-start(f32[2,1,256]{1,0,2:T(2,128)} %get-tuple-element.129), channel_id=1, source_target_pairs={{1,0},{3,2},{5,4},{7,6},{9,8},{11,10},{13,12},{15,14},{17,16},{19,... | collective-permute-start | bytes 6152 | tf_op jit(solution)/shard_map/ppermute | solution.py:20
  20.0 109.3 %collective-permute-start = (f32[2,1,256]{2,0,1:T(2,128)S(1)}, f32[2,1,256]{2,0,1:T(2,128)S(1)}, u32[]{:S(2)}, u32[]{:S(2)}) collective-permute-start(f32[2,1,256]{2,0,1:T(2,128)S(1)} %copy.1640), channel_id=1, source_target_pairs={{0,1},{2,3},{4,5},{6,7},{8,9},{10,11},{12,13},{14,15},{16,17},{18,... | collective-permute-start | bytes 6152 | tf_op jit(solution)/shard_map/ppermute | solution.py:17
  137.7 936.9 %all-gather.10.cloned.1.call-start = ((), (), s32[]{:S(2)}) async-start(), calls=%async_computation.2 | async-start | bytes 1056768 | tf_op jit(solution)/shard_map/all_gather | solution.py:52
  179.9 64.0 %copy-start.2 = (f32[2,128,256]{2,1,0:T(8,128)S(1)}, f32[2,128,256]{2,1,0:T(8,128)}, u32[]{:S(2)}) copy-start(f32[2,128,256]{2,1,0:T(8,128)} %param.5) | copy-start | bytes 786436
  192.5 50.0 %collective-permute-start.2 = (f32[2,1,256]{2,1,0:T(1,128)S(1)}, f32[2,1,256]{2,1,0:T(1,128)S(1)}, u32[]{:S(2)}, u32[]{:S(2)}) collective-permute-start(f32[2,1,256]{2,1,0:T(1,128)S(1)} %get-tuple-element.122), channel_id=1, source_target_pairs={{0,1},{2,3},{4,5},{6,7},{8,9},{10,11},{12,13},{14,15},{16,17},{18,... | collective-permute-start | bytes 6152 | tf_op jit(solution)/shard_map/ppermute | solution.py:17
  194.6 47.9 %collective-permute-start.3 = (f32[2,1,256]{2,1,0:T(1,128)S(1)}, f32[2,1,256]{2,1,0:T(1,128)S(1)}, u32[]{:S(2)}, u32[]{:S(2)}) collective-permute-start(f32[2,1,256]{2,1,0:T(1,128)S(1)} %get-tuple-element.119), channel_id=1, source_target_pairs={{1,0},{3,2},{5,4},{7,6},{9,8},{11,10},{13,12},{15,14},{17,16},{19,... | collective-permute-start | bytes 6152 | tf_op jit(solution)/shard_map/ppermute | solution.py:20
  244.0 26.2 %copy-start.5 = (f32[64,128]{1,0:T(8,128)S(1)}, f32[64,128]{1,0:T(8,128)}, u32[]{:S(2)}) copy-start(f32[64,128]{1,0:T(8,128)} %get-tuple-element.155) | copy-start | bytes 98308
  244.0 375.6 %copy-start.4 = (f32[64,128]{1,0:T(8,128)S(1)}, f32[64,128]{1,0:T(8,128)}, u32[]{:S(2)}) copy-start(f32[64,128]{1,0:T(8,128)} %get-tuple-element.156) | copy-start | bytes 98308
  270.3 349.0 %collective-permute-start.4 = (f32[2,1,128]{2,0,1:T(2,128)S(1)}, f32[2,1,128]{2,0,1:T(2,128)S(1)}, u32[]{:S(2)}, u32[]{:S(2)}) collective-permute-start(f32[2,1,128]{2,0,1:T(2,128)S(1)} %bitcast.453), channel_id=1, source_target_pairs={{0,1},{2,3},{4,5},{6,7},{8,9},{10,11},{12,13},{14,15},{16,17},{18,... | collective-permute-start | bytes 3080 | tf_op jit(solution)/shard_map/ppermute | solution.py:17
  271.7 347.7 %collective-permute-start.5 = (f32[2,1,128]{2,0,1:T(2,128)S(1)}, f32[2,1,128]{2,0,1:T(2,128)S(1)}, u32[]{:S(2)}, u32[]{:S(2)}) collective-permute-start(f32[2,1,128]{2,0,1:T(2,128)S(1)} %bitcast.449), channel_id=1, source_target_pairs={{1,0},{3,2},{5,4},{7,6},{9,8},{11,10},{13,12},{15,14},{17,16},{19,... | collective-permute-start | bytes 3080 | tf_op jit(solution)/shard_map/ppermute | solution.py:20
  619.8 355.7 %collective-permute-start.7 = (f32[2,1,128]{2,0,1:T(2,128)S(1)}, f32[2,1,128]{2,0,1:T(2,128)S(1)}, u32[]{:S(2)}, u32[]{:S(2)}) collective-permute-start(f32[2,1,128]{2,0,1:T(2,128)S(1)} %bitcast.451), channel_id=1, source_target_pairs={{1,0},{3,2},{5,4},{7,6},{9,8},{11,10},{13,12},{15,14},{17,16},{19,... | collective-permute-start | bytes 3080 | tf_op jit(solution)/shard_map/ppermute | solution.py:20
  621.1 354.4 %collective-permute-start.6 = (f32[2,1,128]{2,0,1:T(2,128)S(1)}, f32[2,1,128]{2,0,1:T(2,128)S(1)}, u32[]{:S(2)}, u32[]{:S(2)}) collective-permute-start(f32[2,1,128]{2,0,1:T(2,128)S(1)} %bitcast.447), channel_id=1, source_target_pairs={{0,1},{2,3},{4,5},{6,7},{8,9},{10,11},{12,13},{14,15},{16,17},{18,... | collective-permute-start | bytes 3080 | tf_op jit(solution)/shard_map/ppermute | solution.py:17
  979.7 205.2 %all-gather.12.cloned.1.call-start = ((), (), s32[]{:S(2)}) async-start(), calls=%async_computation.3 | async-start | bytes 1056768 | tf_op jit(solution)/shard_map/all_gather | solution.py:52
  979.8 97.7 %collective-permute-start.8 = (f32[2,1,256]{2,1,0:T(1,128)S(1)}, f32[2,1,256]{2,1,0:T(1,128)S(1)}, u32[]{:S(2)}, u32[]{:S(2)}) collective-permute-start(f32[2,1,256]{2,1,0:T(1,128)S(1)} %get-tuple-element.108), channel_id=1, source_target_pairs={{0,1},{2,3},{4,5},{6,7},{8,9},{10,11},{12,13},{14,15},{16,17},{18,... | collective-permute-start | bytes 6152 | tf_op jit(solution)/shard_map/ppermute | solution.py:17
  981.9 95.7 %collective-permute-start.9 = (f32[2,1,256]{2,1,0:T(1,128)S(1)}, f32[2,1,256]{2,1,0:T(1,128)S(1)}, u32[]{:S(2)}, u32[]{:S(2)}) collective-permute-start(f32[2,1,256]{2,1,0:T(1,128)S(1)} %get-tuple-element.105), channel_id=1, source_target_pairs={{1,0},{3,2},{5,4},{7,6},{9,8},{11,10},{13,12},{15,14},{17,16},{19,... | collective-permute-start | bytes 6152 | tf_op jit(solution)/shard_map/ppermute | solution.py:20
  1083.0 212.5 %all-gather.14.cloned.1.call-start = ((), (), s32[]{:S(2)}) async-start(), calls=%async_computation.4 | async-start | bytes 1056768 | tf_op jit(solution)/shard_map/all_gather | solution.py:52
  1083.1 104.7 %collective-permute-start.10 = (f32[2,1,256]{2,1,0:T(1,128)S(1)}, f32[2,1,256]{2,1,0:T(1,128)S(1)}, u32[]{:S(2)}, u32[]{:S(2)}) collective-permute-start(f32[2,1,256]{2,1,0:T(1,128)S(1)} %get-tuple-element.94), channel_id=1, source_target_pairs={{0,1},{2,3},{4,5},{6,7},{8,9},{10,11},{12,13},{14,15},{16,17},{18,... | collective-permute-start | bytes 6152 | tf_op jit(solution)/shard_map/ppermute | solution.py:17
  1085.1 102.6 %collective-permute-start.11 = (f32[2,1,256]{2,1,0:T(1,128)S(1)}, f32[2,1,256]{2,1,0:T(1,128)S(1)}, u32[]{:S(2)}, u32[]{:S(2)}) collective-permute-start(f32[2,1,256]{2,1,0:T(1,128)S(1)} %get-tuple-element.91), channel_id=1, source_target_pairs={{1,0},{3,2},{5,4},{7,6},{9,8},{11,10},{13,12},{15,14},{17,16},{19,... | collective-permute-start | bytes 6152 | tf_op jit(solution)/shard_map/ppermute | solution.py:20
  1189.8 111.5 %copy-start.3 = (f32[2,128,256]{2,1,0:T(8,128)}, f32[2,128,256]{2,1,0:T(8,128)S(1)}, u32[]{:S(2)}) copy-start(f32[2,128,256]{2,1,0:T(8,128)S(1)} %fusion.13) | copy-start | bytes 786436
  1193.7 104.5 %collective-permute-start.13 = (f32[2,1,256]{2,1,0:T(1,128)S(1)}, f32[2,1,256]{2,1,0:T(1,128)S(1)}, u32[]{:S(2)}, u32[]{:S(2)}) collective-permute-start(f32[2,1,256]{2,1,0:T(1,128)S(1)} %get-tuple-element.77), channel_id=1, source_target_pairs={{1,0},{3,2},{5,4},{7,6},{9,8},{11,10},{13,12},{15,14},{17,16},{19,... | collective-permute-start | bytes 6152 | tf_op jit(solution)/shard_map/ppermute | solution.py:20
  1195.0 103.5 %collective-permute-start.12 = (f32[2,1,256]{2,0,1:T(2,128)S(1)}, f32[2,1,256]{2,0,1:T(2,128)S(1)}, u32[]{:S(2)}, u32[]{:S(2)}) collective-permute-start(f32[2,1,256]{2,0,1:T(2,128)S(1)} %get-tuple-element.80), channel_id=1, source_target_pairs={{0,1},{2,3},{4,5},{6,7},{8,9},{10,11},{12,13},{14,15},{16,17},{18,... | collective-permute-start | bytes 6152 | tf_op jit(solution)/shard_map/ppermute | solution.py:17
Sparse Core Ops, SparseCore 0:
  18.8 105.5 all-gather.5
  137.9 101.6 all-gather.7
  979.8 94.7 all-gather.9
  1083.1 101.6 all-gather.11
  1193.8 101.6 all-gather.13
where the time goes:
time: 1310 us
  blocking collectives  710 us (54%)
  waiting for transfers between devices  421 us (32%)
  local copies, waits for them, and re-layouts  94.2 us (7%)
  other arithmetic  41.1 us (3%)
  starting transfers between devices  26.9 us (2%)
  between operations  15.2 us (1%)
    all_gather x2, blocking collectives, across_sides(): everyone = lax.all_gather(side_rows[None], 'tile', axis=0, tiled=True)  688 us
    all_gather x5, waiting for transfers between devices, across_sides(): everyone = lax.all_gather(side_rows[None], 'tile', axis=0, tiled=True)  421 us
    another operation x2, local copies, waits for them, and re-layouts, body(): noise_terms = jnp.stack([noise_diag[0], noise_diag[1], cross_noise])  27.8 us
    reshape x2, local copies, waits for them, and re-layouts, coarsen_sum(): return values.reshape(new_shape).sum(axis=(-3, -1))  27.8 us
  transfers between devices with their start and end apart: 19, of which 5 were waited for; matrix products, arithmetic and copies ran while one was open for 7% of the time, Pallas kernels for 0%

commit v1 on v0

--- a/solution.py
+++ b/solution.py
@@ -49,7 +49,11 @@
 
 def across_sides(side_rows, link_cols, grid_level):
     if grid_level == "fine":
-        everyone = lax.all_gather(side_rows[None], "tile", axis=0, tiled=True)
+        part = side_rows[None]
+        size = lax.axis_size("tile")
+        blocks = jnp.stack([part for _ in range(size)])
+        blocks = lax.all_to_all(blocks, "tile", split_axis=0, concat_axis=0)
+        everyone = jnp.concatenate(blocks, axis=0)
     else:
         everyone = lax.all_gather(side_rows[None], "tile", axis=0, tiled=True)
     across = everyone[link_cols[0], link_cols[1]]

time: 1310 us -> 1010 us (0.77)
  waiting for transfers between devices: 421 us -> 87.9 us
  starting transfers between devices: 26.9 us -> 79.5 us
  between operations: 15.2 us -> 1.82 us
    all_gather x5 -> x0, waiting for transfers between devices: 421 us -> none  [across_sides(): everyone = lax.all_gather(side_rows[None], 'tile', axis=0, tiled=True)]
    all_to_all x0 -> x5, waiting for transfers between devices: none -> 87.9 us  [across_sides(): blocks = lax.all_to_all(blocks, 'tile', split_axis=0, concat_axis=0)]
    all_to_all x0 -> x5, starting transfers between devices: none -> 44.6 us  [across_sides(): blocks = lax.all_to_all(blocks, 'tile', split_axis=0, concat_axis=0)]
  transfers between devices with their start and end apart: 19 -> 19, of which waited for: 5 -> 4; matrix products, arithmetic and copies ran while one was open for 7% -> 8% of each run, Pallas kernels for 0% -> 0%
where the time goes in v1:
time: 1010 us
  blocking collectives  708 us (70%)
  waiting for transfers between devices  87.9 us (9%)
  local copies, waits for them, and re-layouts  87.2 us (9%)
  starting transfers between devices  79.5 us (8%)
  other arithmetic  48.4 us (5%)
    all_gather x2, blocking collectives, across_sides(): everyone = lax.all_gather(side_rows[None], 'tile', axis=0, tiled=True)  689 us
    all_to_all x5, waiting for transfers between devices, across_sides(): blocks = lax.all_to_all(blocks, 'tile', split_axis=0, concat_axis=0)  87.9 us
    all_to_all x5, starting transfers between devices, across_sides(): blocks = lax.all_to_all(blocks, 'tile', split_axis=0, concat_axis=0)  44.6 us
    another operation x2, local copies, waits for them, and re-layouts, body(): noise_terms = jnp.stack([noise_diag[0], noise_diag[1], cross_noise])  27.8 us
    reshape x2, local copies, waits for them, and re-layouts, coarsen_sum(): return values.reshape(new_shape).sum(axis=(-3, -1))  27.8 us
    ppermute x7, starting transfers between devices, with_halo(): lax.ppermute(lax.slice_in_dim(block, block.shape[dim] - width, None, axis...  25.9 us
    reduce_sum x3, other arithmetic, coarsen_sum(): return values.reshape(new_shape).sum(axis=(-3, -1))  24.6 us
  transfers between devices with their start and end apart: 19, of which 4 were waited for; matrix products, arithmetic and copies ran while one was open for 8% of the time, Pallas kernels for 0%

profile of v1, /device:TPU:2, one launch (start us, length us, event | category | flops | bytes accessed | tf_op | source)
XLA Modules:
  0.0 1012.6 jit_solution(10241292172351659967)
XLA Ops:
  7.2 2.5 psum.49
  11.0 15.6 %all-to-all-start = ((f32[128,1,4,2,256]{4,3,2,1,0:T(2,128)}), f32[128,1,4,2,256]{4,3,2,1,0:T(2,128)S(1)}, u32[]{:S(2)}, u32[]{:S(2)}) async-start(f32[128,1,4,2,256]{4,3,2,1,0:T(2,128)} %stack.213), calls=%async_computation | async-start | bytes 2097152 | tf_op jit(solution)/shard_map/all_to_all | solution.py:55
  27.8 4.4 collective-permute-start
  35.8 20.4 %all-to-all-done = f32[128,1,4,2,256]{4,3,2,1,0:T(2,128)S(1)} async-done(((f32[128,1,4,2,256]{4,3,2,1,0:T(2,128)}), f32[128,1,4,2,256]{4,3,2,1,0:T(2,128)S(1)}, u32[]{:S(2)}, u32[]{:S(2)}) %all-to-all-start) | async-done | bytes 1048608 | tf_op jit(solution)/shard_map/all_to_all | solution.py:55
  62.0 2.5 psum.50
  65.7 7.8 all-to-all-start.1
  73.7 18.1 %stack.220 = f32[2,64,2,128,2]{4,3,2,1,0:T(8,128)} reshape(f32[2,128,256]{2,1,0:T(8,128)S(1)} %copy-done.1) | data formatting | bytes 524288 | tf_op jit(solution)/shard_map/stack | solution.py:138
  91.8 9.7 reshape.589
  101.5 9.7 stack.221
  111.2 4.6 reduce_sum.27
  115.8 12.0 %maximum_reduce_fusion = f32[3,64,128]{2,1,0:T(8,128)S(1)} fusion(f32[1,64,2,128,2]{4,3,2,1,0:T(8,128)} %stack.221, f32[2,64,2,128,2]{4,3,2,1,0:T(8,128)} %stack.220), kind=kLoop, calls=%fused_computation.7 | loop fusion | flops 172032 | bytes 491520 | tf_op jit(solution)/shard_map/reduce_sum | solution.py:43
  129.1 4.4 collective-permute-start.2
  139.9 18.1 %reshape.591 = f32[2,64,2,128,2]{4,3,2,1,0:T(8,128)} reshape(f32[2,128,256]{2,1,0:T(8,128)S(1)} %copy.1203) | data formatting | bytes 524288 | tf_op jit(solution)/shard_map/reshape | solution.py:43
  158.0 8.0 reduce_sum.29
  169.3 3.4 psum.51
  172.8 342.3 %all_gather.6 = f32[128,4,2,128]{3,1,2,0:T(4,128)S(1)} all-gather(f32[1,4,2,128]{3,1,2,0:T(4,128)S(1)} %copy.1206), channel_id=1, replica_groups=mesh['tile'=128,'sub'=2] {'tile'}, dimensions={0}, use_global_device_ids=true | all-gather | bytes 528384 | tf_op jit(solution)/shard_map/all_gather | solution.py:58
  518.2 3.0 collective-permute-start.6
  521.6 2.5 psum.52
  524.1 347.0 %all_gather.7 = f32[128,4,2,128]{3,1,2,0:T(4,128)S(1)} all-gather(f32[1,4,2,128]{3,1,2,0:T(4,128)S(1)} %copy.1214), channel_id=1, replica_groups=mesh['tile'=128,'sub'=2] {'tile'}, dimensions={0}, use_global_device_ids=true | all-gather | bytes 528384 | tf_op jit(solution)/shard_map/all_gather | solution.py:58
  874.1 2.5 psum.53
  877.8 5.3 all-to-all-start.2
  884.4 4.5 collective-permute-start.8
  890.5 22.7 %all-to-all-done.2 = f32[128,1,4,2,256]{4,3,2,1,0:T(2,128)S(1)} async-done(((f32[128,1,4,2,256]{4,3,2,1,0:T(2,128)}), f32[128,1,4,2,256]{4,3,2,1,0:T(2,128)S(1)}, u32[]{:S(2)}, u32[]{:S(2)}) %all-to-all-start.2) | async-done | bytes 1048608 | tf_op jit(solution)/shard_map/all_to_all | solution.py:55
  918.8 2.5 psum.54
  922.6 7.8 all-to-all-start.3
  931.6 4.5 collective-permute-start.10
  937.7 22.3 %all-to-all-done.3 = f32[128,1,4,2,256]{4,3,2,1,0:T(2,128)S(1)} async-done(((f32[128,1,4,2,256]{4,3,2,1,0:T(2,128)}), f32[128,1,4,2,256]{4,3,2,1,0:T(2,128)S(1)}, u32[]{:S(2)}, u32[]{:S(2)}) %all-to-all-start.3) | async-done | bytes 1048608 | tf_op jit(solution)/shard_map/all_to_all | solution.py:55
  965.6 2.5 psum.55
  969.4 8.1 all-to-all-start.4
  978.8 3.7 collective-permute-start.12
  984.7 22.5 %all-to-all-done.4 = f32[128,1,4,2,256]{4,3,2,1,0:T(2,128)S(1)} async-done(((f32[128,1,4,2,256]{4,3,2,1,0:T(2,128)}), f32[128,1,4,2,256]{4,3,2,1,0:T(2,128)S(1)}, u32[]{:S(2)}, u32[]{:S(2)}) %all-to-all-start.4) | async-done | bytes 1048608 | tf_op jit(solution)/shard_map/all_to_all | solution.py:55
  1009.5 1.9 fusion.17
  (235 shorter events, 64.0 us)
Async XLA Ops:
  0.6 73.1 %copy-start.1 = (f32[2,128,256]{2,1,0:T(8,128)S(1)}, f32[2,128,256]{2,1,0:T(8,128)}, u32[]{:S(2)}) copy-start(f32[2,128,256]{2,1,0:T(8,128)} %param.7) | copy-start | bytes 786436
  11.0 80.8 %copy-start = (f32[128,256]{1,0:T(8,128)S(1)}, f32[128,256]{1,0:T(8,128)}, u32[]{:S(2)}) copy-start(f32[128,256]{1,0:T(8,128)} %param.6) | copy-start | bytes 393220
  11.0 45.2 %all-to-all-start = ((f32[128,1,4,2,256]{4,3,2,1,0:T(2,128)}), f32[128,1,4,2,256]{4,3,2,1,0:T(2,128)S(1)}, u32[]{:S(2)}, u32[]{:S(2)}) async-start(f32[128,1,4,2,256]{4,3,2,1,0:T(2,128)} %stack.213), calls=%async_computation | async-start | bytes 2097152 | tf_op jit(solution)/shard_map/all_to_all | solution.py:55
  26.5 30.9 %collective-permute-start.1 = (f32[2,1,256]{1,2,0:T(8,128)}, f32[2,1,256]{1,2,0:T(8,128)}, u32[]{:S(2)}, u32[]{:S(2)}) collective-permute-start(f32[2,1,256]{1,2,0:T(8,128)} %get-tuple-element.118), channel_id=1, source_target_pairs={{1,0},{3,2},{5,4},{7,6},{9,8},{11,10},{13,12},{15,14},{17,16},{19,... | collective-permute-start | bytes 6152 | tf_op jit(solution)/shard_map/ppermute | solution.py:20
  27.8 30.6 %collective-permute-start = (f32[2,1,256]{1,2,0:T(8,128)}, f32[2,1,256]{1,2,0:T(8,128)}, u32[]{:S(2)}, u32[]{:S(2)}) collective-permute-start(f32[2,1,256]{1,2,0:T(8,128)} %get-tuple-element.119), channel_id=1, source_target_pairs={{0,1},{2,3},{4,5},{6,7},{8,9},{10,11},{12,13},{14,15},{16,17},{18,... | collective-permute-start | bytes 6152 | tf_op jit(solution)/shard_map/ppermute | solution.py:17
  65.7 69.4 %all-to-all-start.1 = ((f32[128,1,4,2,256]{4,3,2,1,0:T(2,128)}), f32[128,1,4,2,256]{4,3,2,1,0:T(2,128)S(1)}, u32[]{:S(2)}, u32[]{:S(2)}) async-start(f32[128,1,4,2,256]{4,3,2,1,0:T(2,128)} %stack.226), calls=%async_computation.1 | async-start | bytes 2097152 | tf_op jit(solution)/shard_map/all_to_all | solution.py:55
  111.2 16.6 %copy-start.2 = (f32[2,1,256]{1,2,0:T(8,128)S(1)}, f32[2,1,256]{1,2,0:T(8,128)}, u32[]{:S(2)}) copy-start(f32[2,1,256]{1,2,0:T(8,128)} %get-tuple-element.108) | copy-start | bytes 6148
  127.8 8.6 collective-permute-start.3
  129.1 8.2 collective-permute-start.2
  166.2 350.2 %collective-permute-start.4 = (f32[2,1,128]{2,0,1:T(2,128)S(1)}, f32[2,1,128]{2,0,1:T(2,128)S(1)}, u32[]{:S(2)}, u32[]{:S(2)}) collective-permute-start(f32[2,1,128]{2,0,1:T(2,128)S(1)} %bitcast.499), channel_id=1, source_target_pairs={{0,1},{2,3},{4,5},{6,7},{8,9},{10,11},{12,13},{14,15},{16,17},{18,... | collective-permute-start | bytes 3080 | tf_op jit(solution)/shard_map/ppermute | solution.py:17
  167.6 348.9 %collective-permute-start.5 = (f32[2,1,128]{2,0,1:T(2,128)S(1)}, f32[2,1,128]{2,0,1:T(2,128)S(1)}, u32[]{:S(2)}, u32[]{:S(2)}) collective-permute-start(f32[2,1,128]{2,0,1:T(2,128)S(1)} %bitcast.495), channel_id=1, source_target_pairs={{1,0},{3,2},{5,4},{7,6},{9,8},{11,10},{13,12},{15,14},{17,16},{19,... | collective-permute-start | bytes 3080 | tf_op jit(solution)/shard_map/ppermute | solution.py:20
  516.9 355.7 %collective-permute-start.7 = (f32[2,1,128]{2,0,1:T(2,128)S(1)}, f32[2,1,128]{2,0,1:T(2,128)S(1)}, u32[]{:S(2)}, u32[]{:S(2)}) collective-permute-start(f32[2,1,128]{2,0,1:T(2,128)S(1)} %bitcast.497), channel_id=1, source_target_pairs={{1,0},{3,2},{5,4},{7,6},{9,8},{11,10},{13,12},{15,14},{17,16},{19,... | collective-permute-start | bytes 3080 | tf_op jit(solution)/shard_map/ppermute | solution.py:20
  518.2 354.4 %collective-permute-start.6 = (f32[2,1,128]{2,0,1:T(2,128)S(1)}, f32[2,1,128]{2,0,1:T(2,128)S(1)}, u32[]{:S(2)}, u32[]{:S(2)}) collective-permute-start(f32[2,1,128]{2,0,1:T(2,128)S(1)} %bitcast.493), channel_id=1, source_target_pairs={{0,1},{2,3},{4,5},{6,7},{8,9},{10,11},{12,13},{14,15},{16,17},{18,... | collective-permute-start | bytes 3080 | tf_op jit(solution)/shard_map/ppermute | solution.py:17
  877.8 35.3 %all-to-all-start.2 = ((f32[128,1,4,2,256]{4,3,2,1,0:T(2,128)}), f32[128,1,4,2,256]{4,3,2,1,0:T(2,128)S(1)}, u32[]{:S(2)}, u32[]{:S(2)}) async-start(f32[128,1,4,2,256]{4,3,2,1,0:T(2,128)} %stack.244), calls=%async_computation.2 | async-start | bytes 2097152 | tf_op jit(solution)/shard_map/all_to_all | solution.py:55
  883.1 31.2 %collective-permute-start.9 = (f32[2,1,256]{1,2,0:T(8,128)S(1)}, f32[2,1,256]{1,2,0:T(8,128)}, u32[]{:S(2)}, u32[]{:S(2)}) collective-permute-start(f32[2,1,256]{1,2,0:T(8,128)S(1)} %get-tuple-element.96), channel_id=1, source_target_pairs={{1,0},{3,2},{5,4},{7,6},{9,8},{11,10},{13,12},{15,14},{17,16},{19,... | collective-permute-start | bytes 6152 | tf_op jit(solution)/shard_map/ppermute | solution.py:20
  884.4 30.9 %collective-permute-start.8 = (f32[2,1,256]{1,2,0:T(8,128)}, f32[2,1,256]{1,2,0:T(8,128)}, u32[]{:S(2)}, u32[]{:S(2)}) collective-permute-start(f32[2,1,256]{1,2,0:T(8,128)} %get-tuple-element.97), channel_id=1, source_target_pairs={{0,1},{2,3},{4,5},{6,7},{8,9},{10,11},{12,13},{14,15},{16,17},{18,... | collective-permute-start | bytes 6152 | tf_op jit(solution)/shard_map/ppermute | solution.py:17
  922.6 37.4 %all-to-all-start.3 = ((f32[128,1,4,2,256]{4,3,2,1,0:T(2,128)}), f32[128,1,4,2,256]{4,3,2,1,0:T(2,128)S(1)}, u32[]{:S(2)}, u32[]{:S(2)}) async-start(f32[128,1,4,2,256]{4,3,2,1,0:T(2,128)} %stack.254), calls=%async_computation.3 | async-start | bytes 2097152 | tf_op jit(solution)/shard_map/all_to_all | solution.py:55
  930.3 30.9 %collective-permute-start.11 = (f32[2,1,256]{1,2,0:T(8,128)S(1)}, f32[2,1,256]{1,2,0:T(8,128)}, u32[]{:S(2)}, u32[]{:S(2)}) collective-permute-start(f32[2,1,256]{1,2,0:T(8,128)S(1)} %get-tuple-element.88), channel_id=1, source_target_pairs={{1,0},{3,2},{5,4},{7,6},{9,8},{11,10},{13,12},{15,14},{17,16},{19,... | collective-permute-start | bytes 6152 | tf_op jit(solution)/shard_map/ppermute | solution.py:20
  931.6 30.6 %collective-permute-start.10 = (f32[2,1,256]{1,2,0:T(8,128)}, f32[2,1,256]{1,2,0:T(8,128)}, u32[]{:S(2)}, u32[]{:S(2)}) collective-permute-start(f32[2,1,256]{1,2,0:T(8,128)} %get-tuple-element.89), channel_id=1, source_target_pairs={{0,1},{2,3},{4,5},{6,7},{8,9},{10,11},{12,13},{14,15},{16,17},{18,... | collective-permute-start | bytes 6152 | tf_op jit(solution)/shard_map/ppermute | solution.py:17
  969.4 37.8 %all-to-all-start.4 = ((f32[128,1,4,2,256]{4,3,2,1,0:T(2,128)}), f32[128,1,4,2,256]{4,3,2,1,0:T(2,128)S(1)}, u32[]{:S(2)}, u32[]{:S(2)}) async-start(f32[128,1,4,2,256]{4,3,2,1,0:T(2,128)} %stack.264), calls=%async_computation.4 | async-start | bytes 2097152 | tf_op jit(solution)/shard_map/all_to_all | solution.py:55
  977.5 31.0 %collective-permute-start.13 = (f32[2,1,256]{1,0,2:T(2,128)S(1)}, f32[2,1,256]{1,0,2:T(2,128)}, u32[]{:S(2)}, u32[]{:S(2)}) collective-permute-start(f32[2,1,256]{1,0,2:T(2,128)S(1)} %get-tuple-element.82), channel_id=1, source_target_pairs={{1,0},{3,2},{5,4},{7,6},{9,8},{11,10},{13,12},{15,14},{17,16},{19,... | collective-permute-start | bytes 6152 | tf_op jit(solution)/shard_map/ppermute | solution.py:20
  978.8 29.2 %collective-permute-start.12 = (f32[2,1,256]{2,0,1:T(2,128)S(1)}, f32[2,1,256]{2,0,1:T(2,128)S(1)}, u32[]{:S(2)}, u32[]{:S(2)}) collective-permute-start(f32[2,1,256]{2,0,1:T(2,128)S(1)} %copy.1267), channel_id=1, source_target_pairs={{0,1},{2,3},{4,5},{6,7},{8,9},{10,11},{12,13},{14,15},{16,17},{18,... | collective-permute-start | bytes 6152 | tf_op jit(solution)/shard_map/ppermute | solution.py:17
